TPU v7x, 32 devices: a whole 2x2x4 slice. The times are simulated.
32 devices in a mesh: tm: 4 (over y, x), space: 8 (over z, core).
Axes of the slice: x: 2, y: 2, z: 4, core: 2. Of those that a mesh axis runs over, the one named last changes fastest.
Arguments:
- frames_in: bfloat16 [32, 512, 1024], P('tm', 'space'), may hold values from -6 to 6
- time_gain: float32 [1024], replicated, may hold values from 0.1 to 1.9
- time_shift: float32 [1024], replicated, may hold values from -4 to 4
- time_query: bfloat16 [1024, 1024], replicated
- time_key: bfloat16 [1024, 1024], replicated
- time_value: bfloat16 [1024, 1024], replicated, may hold values from -0.1875 to 0.1875
- time_out: bfloat16 [1024, 1024], replicated, may hold values from -0.1875 to 0.1875
- space_gain: float32 [1024], replicated, may hold values from 0.1 to 1.9
- space_shift: float32 [1024], replicated, may hold values from -4 to 4
- space_query: bfloat16 [1024, 1024], replicated
- space_key: bfloat16 [1024, 1024], replicated
- space_value: bfloat16 [1024, 1024], replicated, may hold values from -0.1875 to 0.1875
- space_out: bfloat16 [1024, 1024], replicated, may hold values from -0.1875 to 0.1875
Outputs:
- frames_out: bfloat16 [32, 512, 1024], P('tm', 'space')
All inputs are finite; a program needn't handle non-finite values.
Results may differ from a plain program's by a relative error of at most 0.03.
Values may be sent and summed in bfloat16 or wider, within the bound.
A program may use at most 192 MiB of HBM per device.

v0:
```python
import jax
import jax.numpy as jnp
from jax import lax
from jax.sharding import PartitionSpec as P

HEAD_DIM = 64


def layer_norm(tokens, gain, shift):
    values = tokens.astype(jnp.float32)
    mean_value = jnp.mean(values, axis=-1, keepdims=True)
    variance = jnp.mean((values - mean_value) ** 2, axis=-1, keepdims=True)
    return ((values - mean_value) * lax.rsqrt(variance + 1e-05) * gain + shift).astype(jnp.bfloat16)


def project(tokens, weight):
    return jnp.dot(tokens, weight, preferred_element_type=jnp.float32)


def split_heads(tokens):
    return tokens.reshape(tokens.shape[0], tokens.shape[1], tokens.shape[2] // HEAD_DIM, HEAD_DIM)


def attend_frames(queries, keys_in, values_in):
    shape = queries.shape
    scores = (
        jnp.einsum(
            "qphd,kphd->phqk",
            split_heads(queries),
            split_heads(keys_in),
            preferred_element_type=jnp.float32,
        )
        * 0.125
    )
    weights = jax.nn.softmax(scores, axis=-1).astype(jnp.bfloat16)
    result = jnp.einsum(
        "phqk,kphd->qphd", weights, split_heads(values_in), preferred_element_type=jnp.float32
    )
    return result.astype(jnp.bfloat16).reshape(shape)


def to_slots(tokens, slots):
    return tokens.reshape(tokens.shape[0], slots, tokens.shape[1] // slots, tokens.shape[2])


def flat_items(piece):
    return piece.reshape(piece.shape[0], piece.shape[1] * piece.shape[2], piece.shape[3])


def body(
    frames_in,
    time_gain,
    time_shift,
    time_query,
    time_key,
    time_value,
    time_out,
    space_gain,
    space_shift,
    space_query,
    space_key,
    space_value,
    space_out,
):
    slots = lax.axis_size("tm")
    frame_rows, patch_rows, width = frames_in.shape
    normed = layer_norm(frames_in, time_gain, time_shift)
    projected = tuple(
        (
            to_slots(project(normed, weight).astype(jnp.bfloat16), slots)
            for weight in (time_query, time_key, time_value)
        )
    )
    pieces = (
        lax.all_to_all(projected[0], "tm", split_axis=1, concat_axis=0, tiled=True),
        lax.all_to_all(projected[1], "tm", split_axis=1, concat_axis=0, tiled=True),
        lax.all_to_all(projected[2], "tm", split_axis=1, concat_axis=0, tiled=True),
    )
    shape = pieces[0].shape
    result = attend_frames(flat_items(pieces[0]), flat_items(pieces[1]), flat_items(pieces[2]))
    attended = result.reshape(shape)
    returned = lax.all_to_all(attended, "tm", split_axis=0, concat_axis=1, tiled=True).reshape(
        frame_rows, patch_rows, width
    )
    after_time = (frames_in.astype(jnp.float32) + project(returned, time_out)).astype(jnp.bfloat16)
    normed = layer_norm(after_time, space_gain, space_shift)
    space_queries = project(normed, space_query).astype(jnp.bfloat16)
    space_keys = project(normed, space_key).astype(jnp.bfloat16)
    space_values = project(normed, space_value).astype(jnp.bfloat16)
    query_heads = split_heads(space_queries)
    frame_count, patch_count, head_count, head_size = query_heads.shape
    running_max = jnp.full((frame_count, head_count, patch_count), -1e30, jnp.float32)
    pieces = (
        lax.all_gather(space_keys, "space", axis=1, tiled=True),
        lax.all_gather(space_values, "space", axis=1, tiled=True),
    )
    scores = (
        jnp.einsum(
            "fqhd,fkhd->fhqk",
            query_heads,
            split_heads(pieces[0]),
            preferred_element_type=jnp.float32,
        )
        * 0.125
    )
    new_max = jnp.maximum(running_max, jnp.max(scores, axis=-1))
    weights = jnp.exp(scores - new_max[..., None])
    new_sum = jnp.sum(weights, axis=-1)
    added = jnp.einsum(
        "fhqk,fkhd->fqhd",
        weights.astype(jnp.bfloat16),
        split_heads(pieces[1]),
        preferred_element_type=jnp.float32,
    )
    spatial = (added / jnp.transpose(new_sum, (0, 2, 1))[..., None]).astype(jnp.bfloat16)
    spatial = spatial.reshape(frame_count, patch_count, head_count * head_size)
    return (after_time.astype(jnp.float32) + project(spatial, space_out)).astype(jnp.bfloat16)


def solution(mesh):
    return jax.shard_map(
        body,
        mesh=mesh,
        in_specs=(
            P("tm", "space", None),
            P(),
            P(),
            P(),
            P(),
            P(),
            P(),
            P(),
            P(),
            P(),
            P(),
            P(),
            P(),
        ),
        out_specs=P("tm", "space", None),
        check_vma=False,
    )
```

profile of v0, /device:TPU:0, one launch (start us, length us, event | category | flops | bytes accessed | tf_op | source)
XLA Modules:
  0.0 297.2 jit_solution(11716532837068513903)
XLA Ops:
  6.5 0.0 copy-start
  6.5 1.6 convert_reduce_fusion.1
  8.1 1.6 fusion.21
  9.8 0.0 copy-done.6
  9.8 0.0 copy-done.11
  9.8 0.0 copy-done.10
  9.8 2.9 fusion.57
  12.8 1.1 copy.33
  13.8 5.2 %all-to-all-start.1 = ((bf16[8,4,16,1024]{3,2,0,1:T(8,128)(2,1)}), bf16[8,4,16,1024]{3,2,0,1:T(8,128)(2,1)S(1)}, u32[]{:S(2)}, u32[]{:S(2)}) async-start(bf16[8,4,16,1024]{3,2,0,1:T(8,128)(2,1)} %copy.33), calls=%async_computation.1 | async-start | bytes 2097152 | tf_op jit(solution)/shard_map/all_to_all | solution.py:75
  19.0 3.2 %fusion.60 = bf16[8,64,1024]{2,1,0:T(8,128)(2,1)S(1)} fusion(bf16[1024,1024]{1,0:T(8,128)(2,1)} %param.17, bf16[8,64,1024]{2,1,0:T(8,128)(2,1)} %param.13, f32[1024]{0:T(1024)S(1)} %copy-done.10, f32[1024]{0:T(1024)S(1)} %copy-done.11, f32[8,64]{1,0:T(8,128)S(1)} %add_rsqrt_fusion.1, f32[8,64]{1,0:T(8,128)S(1)} %broadcast_multiply_fusion.1), kind=kOutput, calls=%fused_computation.62 | convolution fusion | flops 1077411840 | bytes 4206592 | tf_op jit(solution)/shard_map/dot_general | solution.py:17
  22.2 1.0 copy.34
  23.3 9.3 %all-to-all-done.1 = bf16[8,4,16,1024]{3,2,0,1:T(8,128)(2,1)S(1)} async-done(((bf16[8,4,16,1024]{3,2,0,1:T(8,128)(2,1)}), bf16[8,4,16,1024]{3,2,0,1:T(8,128)(2,1)S(1)}, u32[]{:S(2)}, u32[]{:S(2)}) %all-to-all-start.1) | async-done | bytes 1048608 | tf_op jit(solution)/shard_map/all_to_all | solution.py:75
  32.6 1.0 copy-done.5
  33.6 3.5 %all-to-all-start.2 = ((bf16[8,4,16,1024]{3,2,0,1:T(8,128)(2,1)}), bf16[8,4,16,1024]{3,2,0,1:T(8,128)(2,1)S(1)}, u32[]{:S(2)}, u32[]{:S(2)}) async-start(bf16[8,4,16,1024]{3,2,0,1:T(8,128)(2,1)} %copy.34), calls=%async_computation.2 | async-start | bytes 2097152 | tf_op jit(solution)/shard_map/all_to_all | solution.py:76
  37.2 3.2 %fusion.54 = bf16[8,64,1024]{2,1,0:T(8,128)(2,1)S(1)} fusion(bf16[1024,1024]{1,0:T(8,128)(2,1)} %param.18, bf16[8,64,1024]{2,1,0:T(8,128)(2,1)} %param.13, f32[1024]{0:T(1024)S(1)} %copy-done.10, f32[1024]{0:T(1024)S(1)} %copy-done.11, f32[8,64]{1,0:T(8,128)S(1)} %add_rsqrt_fusion.1, f32[8,64]{1,0:T(8,128)S(1)} %broadcast_multiply_fusion.1), kind=kOutput, calls=%fused_computation.60 | convolution fusion | flops 1077411840 | bytes 4206592 | tf_op jit(solution)/shard_map/dot_general | solution.py:17
  40.4 1.1 copy.32
  41.4 4.0 %reshape_reshape.13 = bf16[32,16,16,64]{3,2,1,0:T(8,128)(2,1)} reshape(bf16[4,8,1,16,1024]{4,3,1,0,2:T(8,128)(2,1)} %bitcast.91) | data formatting | bytes 2097152 | tf_op jit(solution)/shard_map/reshape;reshape | solution.py:21
  45.5 4.8 %all-to-all-done.2 = bf16[8,4,16,1024]{3,2,0,1:T(8,128)(2,1)S(1)} async-done(((bf16[8,4,16,1024]{3,2,0,1:T(8,128)(2,1)}), bf16[8,4,16,1024]{3,2,0,1:T(8,128)(2,1)S(1)}, u32[]{:S(2)}, u32[]{:S(2)}) %all-to-all-start.2) | async-done | bytes 1048608 | tf_op jit(solution)/shard_map/all_to_all | solution.py:76
  50.3 4.2 %all-to-all-start = ((bf16[8,4,16,1024]{3,2,0,1:T(8,128)(2,1)}), bf16[8,4,16,1024]{3,2,0,1:T(8,128)(2,1)}, u32[]{:S(2)}, u32[]{:S(2)}) async-start(bf16[8,4,16,1024]{3,2,0,1:T(8,128)(2,1)} %copy.32), calls=%async_computation | async-start | bytes 2097152 | tf_op jit(solution)/shard_map/all_to_all | solution.py:77
  54.5 0.2 all-gather.5.cloned.1.call-start
  54.7 2.3 reshape_reshape.14
  57.1 4.9 %fusion.47 = f32[16,16,32,32]{2,3,1,0:T(8,128)S(1)} fusion(bf16[32,16,16,64]{3,2,1,0:T(8,128)(2,1)} %reshape_reshape.14, bf16[32,16,16,64]{3,2,1,0:T(8,128)(2,1)} %reshape_reshape.13), kind=kOutput, calls=%fused_computation.54 | convolution fusion | flops 33554432 | bytes 3145728 | tf_op jit(solution)/shard_map/qphd,kphd->phqk/dot_general | solution.py:27
  62.0 3.2 %fusion.84 = (f32[16,16,32]{2,1,0:T(8,128)S(1)}, f32[16,16,32,32]{2,3,1,0:T(8,128)}) fusion(f32[16,16,32,32]{2,3,1,0:T(8,128)S(1)} %fusion.47), kind=kOutput, calls=%fused_computation.73 | output fusion | flops 1048607 | bytes 2129920 | tf_op jit(solution)/shard_map/sub | solution.py:35
  65.2 2.5 all-to-all-done
  67.7 4.0 %reshape_reshape.12 = bf16[32,16,16,64]{3,2,1,0:T(8,128)(2,1)} reshape(bf16[4,8,1,16,1024]{4,3,1,0,2:T(8,128)(2,1)} %bitcast.3) | data formatting | bytes 2097152 | tf_op jit(solution)/shard_map/reshape;reshape | solution.py:21
  71.7 4.6 %convert_bitcast_fusion = bf16[32,16,16,64]{3,0,2,1:T(8,128)(2,1)S(1)} fusion(f32[16,16,32,32]{2,3,1,0:T(8,128)} %get-tuple-element.6, f32[16,16,32]{2,1,0:T(8,128)S(1)} %get-tuple-element.5, bf16[32,16,16,64]{3,2,1,0:T(8,128)(2,1)} %reshape_reshape.12), kind=kOutput, calls=%fused_computation.57 | convolution fusion | flops 34603008 | bytes 3178496 | tf_op jit(solution)/shard_map/phqk,kphd->qphd/dot_general | solution.py:36
  76.4 2.2 copy.39
  78.5 3.2 %reshape_reshape.15 = bf16[32,1,16,1024]{3,2,0,1:T(8,128)(2,1)S(1)} reshape(bf16[32,16,16,64]{3,2,1,0:T(8,128)(2,1)} %copy.39) | data formatting | bytes 2097152 | tf_op jit(solution)/shard_map/reshape;reshape | solution.py:81
  81.8 0.0 copy-start.7
  81.8 16.2 %all_to_all.60 = bf16[32,1,16,1024]{3,2,1,0:T(8,128)(2,1)S(1)} all-to-all(bf16[32,1,16,1024]{3,2,1,0:T(8,128)(2,1)S(1)} %bitcast.92), channel_id=1, replica_groups=mesh['tm'=4,'space'=8] {'tm'}, dimensions={0} | all-to-all | bytes 2097152 | tf_op jit(solution)/shard_map/all_to_all | solution.py:82
  98.0 0.1 copy.41
  98.1 0.0 copy-done
  98.1 0.0 copy-done.7
  98.1 0.0 copy-start.9
  98.1 0.0 copy-start.12
  98.1 0.0 copy-start.13
  98.1 1.4 convert_reduce_fusion
  99.5 0.0 copy-start.3
  99.5 0.4 fusion.17
  99.9 0.0 copy-done.9
  100.0 0.0 copy-done.12
  100.0 0.0 copy-done.13
  100.0 2.3 fusion.69
  102.3 0.0 all-gather.5.cloned.1.call-update
  102.3 0.0 all-gather.3.cloned.1.call-start
  102.4 3.9 %fusion.63 = bf16[8,64,1024]{2,1,0:T(8,128)(2,1)} fusion(bf16[1024,1024]{1,0:T(8,128)(2,1)} %param.24, bf16[8,64,1024]{2,1,0:T(8,128)(2,1)S(1)} %get-tuple-element.8, f32[1024]{0:T(1024)S(1)} %copy-done.12, f32[1024]{0:T(1024)S(1)} %copy-done.13, f32[8,64]{1,0:T(8,128)S(1)} %add_rsqrt_fusion, f32[8,64]{1,0:T(8,128)S(1)} %broadcast_multiply_fusion), kind=kOutput, calls=%fused_computation.63 | convolution fusion | flops 1077411840 | bytes 4206592 | tf_op jit(solution)/shard_map/dot_general | solution.py:17
  106.3 0.0 all-gather.3.cloned.1.call-update
  106.4 0.0 copy-done.3
  106.4 3.9 %fusion.66 = bf16[8,64,1024]{2,1,0:T(8,128)(2,1)} fusion(bf16[1024,1024]{1,0:T(8,128)(2,1)} %param.22, bf16[8,64,1024]{2,1,0:T(8,128)(2,1)S(1)} %get-tuple-element.8, f32[1024]{0:T(1024)S(1)} %copy-done.12, f32[1024]{0:T(1024)S(1)} %copy-done.13, f32[8,64]{1,0:T(8,128)S(1)} %add_rsqrt_fusion, f32[8,64]{1,0:T(8,128)S(1)} %broadcast_multiply_fusion), kind=kOutput, calls=%fused_computation.64 | convolution fusion | flops 1077411840 | bytes 4206592 | tf_op jit(solution)/shard_map/dot_general | solution.py:17
  110.2 3.0 %reshape.67 = bf16[8,64,16,64]{3,2,1,0:T(8,128)(2,1)S(1)} reshape(bf16[8,64,1024]{2,1,0:T(8,128)(2,1)} %fusion.66) | data formatting | bytes 2097152 | tf_op jit(solution)/shard_map/reshape | solution.py:21
  113.2 71.1 %all-gather.5.cloned.1.call-done = bf16[8,512,1024]{2,1,0:T(8,128)(2,1)} async-done(((bf16[8,64,1024]{2,1,0:T(8,128)(2,1)}), bf16[8,512,1024]{2,1,0:T(8,128)(2,1)}) %all-gather.5.cloned.1.call-update) | async-done | bytes 8388624 | tf_op jit(solution)/shard_map/all_gather | solution.py:94
  184.3 11.7 %copy.43 = bf16[8,512,1024]{1,2,0:T(8,128)(2,1)} copy(bf16[8,512,1024]{2,1,0:T(8,128)(2,1)} %all-gather.5.cloned.1.call-done) | data formatting | bytes 16777216 | tf_op jit(solution)/shard_map/all_gather | solution.py:94
  196.0 4.9 %multiply_reduce_fusion = (f32[8,16,64]{2,1,0:T(8,128)S(1)}, f32[8,16,64,512]{3,2,1,0:T(8,128)S(1)}) fusion(bf16[8,512,16,64]{1,3,2,0:T(8,128)(2,1)} %bitcast.87, bf16[8,64,16,64]{3,2,1,0:T(8,128)(2,1)S(1)} %reshape.67), kind=kOutput, calls=%fused_computation.2 | convolution fusion | flops 545251328 | bytes 26247168 | tf_op jit(solution)/shard_map/fqhd,fkhd->fhqk/dot_general | solution.py:98
  200.8 0.0 copy-start.2
  200.9 5.7 %copy-done.2 = f32[8,16,64,512]{3,2,1,0:T(8,128)} copy-done((f32[8,16,64,512]{3,2,1,0:T(8,128)}, f32[8,16,64,512]{3,2,1,0:T(8,128)S(1)}, u32[]{:S(2)}) %copy-start.2) | copy-done | bytes 16777240
  206.6 4.2 %fusion.1 = f32[8,16,64]{2,1,0:T(8,128)S(1)} fusion(f32[8,16,64,512]{3,2,1,0:T(8,128)S(1)} %get-tuple-element.10, f32[8,16,64]{2,1,0:T(8,128)S(1)} %broadcast_maximum_fusion), kind=kLoop, calls=%fused_computation.3 | loop fusion | flops 12574720 | bytes 16842752 | tf_op jit(solution)/shard_map/reduce_sum | solution.py:108
  210.7 55.7 %all-gather.3.cloned.1.call-done = bf16[8,512,1024]{2,1,0:T(8,128)(2,1)} async-done(((bf16[8,64,1024]{2,1,0:T(8,128)(2,1)}), bf16[8,512,1024]{2,1,0:T(8,128)(2,1)}) %all-gather.3.cloned.1.call-update) | async-done | bytes 8388624 | tf_op jit(solution)/shard_map/all_gather | solution.py:95
  266.5 11.4 %copy.42 = bf16[8,512,1024]{1,2,0:T(8,128)(2,1)} copy(bf16[8,512,1024]{2,1,0:T(8,128)(2,1)} %all-gather.3.cloned.1.call-done) | data formatting | bytes 16777216 | tf_op jit(solution)/shard_map/all_gather | solution.py:95
  277.9 10.2 %fusion.7 = bf16[8,64,16,64]{1,3,2,0:T(8,128)(2,1)S(1)} fusion(bf16[8,512,16,64]{1,3,2,0:T(8,128)(2,1)} %bitcast.88, f32[8,16,64,512]{3,2,1,0:T(8,128)} %copy-done.2, f32[8,16,64]{2,1,0:T(8,128)S(1)} %broadcast_maximum_fusion, f32[8,64,16]{1,2,0:T(8,128)S(1)} %bitcast.98), kind=kOutput, calls=%fused_computation.9 | convolution fusion | flops 550502400 | bytes 26279936 | tf_op jit(solution)/shard_map/fhqk,fkhd->fqhd/dot_general | solution.py:109
  288.1 0.0 copy-done.4
  288.1 0.0 copy-done.8
  288.1 0.0 copy-start.1
  288.1 2.3 fusion.26
  290.3 0.0 copy-done.1
  (11 shorter events, 0.0 us)
Async XLA Ops:
  6.5 91.6 %copy-start = (bf16[1024,1024]{1,0:T(8,128)(2,1)S(1)}, bf16[1024,1024]{1,0:T(8,128)(2,1)}, u32[]{:S(2)}) copy-start(bf16[1024,1024]{1,0:T(8,128)(2,1)} %param.19) | copy-start | bytes 6291460
  6.5 3.3 %copy-start.6 = (bf16[8,64,1024]{2,1,0:T(8,128)(2,1)S(1)}, bf16[8,64,1024]{2,1,0:T(8,128)(2,1)}, u32[]{:S(2)}) copy-start(bf16[8,64,1024]{2,1,0:T(8,128)(2,1)} %param.13) | copy-start | bytes 3145732
  6.5 3.3 %copy-start.11 = (f32[1024]{0:T(1024)S(1)}, f32[1024]{0:T(1024)}, u32[]{:S(2)}) copy-start(f32[1024]{0:T(1024)} %param.14) | copy-start | bytes 12292
  6.5 3.3 %copy-start.10 = (f32[1024]{0:T(1024)S(1)}, f32[1024]{0:T(1024)}, u32[]{:S(2)}) copy-start(f32[1024]{0:T(1024)} %param.15) | copy-start | bytes 12292
  13.8 18.8 %all-to-all-start.1 = ((bf16[8,4,16,1024]{3,2,0,1:T(8,128)(2,1)}), bf16[8,4,16,1024]{3,2,0,1:T(8,128)(2,1)S(1)}, u32[]{:S(2)}, u32[]{:S(2)}) async-start(bf16[8,4,16,1024]{3,2,0,1:T(8,128)(2,1)} %copy.33), calls=%async_computation.1 | async-start | bytes 2097152 | tf_op jit(solution)/shard_map/all_to_all | solution.py:75
  32.6 1.0 copy-start.5
  33.6 16.6 %all-to-all-start.2 = ((bf16[8,4,16,1024]{3,2,0,1:T(8,128)(2,1)}), bf16[8,4,16,1024]{3,2,0,1:T(8,128)(2,1)S(1)}, u32[]{:S(2)}, u32[]{:S(2)}) async-start(bf16[8,4,16,1024]{3,2,0,1:T(8,128)(2,1)} %copy.34), calls=%async_computation.2 | async-start | bytes 2097152 | tf_op jit(solution)/shard_map/all_to_all | solution.py:76
  50.3 17.4 %all-to-all-start = ((bf16[8,4,16,1024]{3,2,0,1:T(8,128)(2,1)}), bf16[8,4,16,1024]{3,2,0,1:T(8,128)(2,1)}, u32[]{:S(2)}, u32[]{:S(2)}) async-start(bf16[8,4,16,1024]{3,2,0,1:T(8,128)(2,1)} %copy.32), calls=%async_computation | async-start | bytes 2097152 | tf_op jit(solution)/shard_map/all_to_all | solution.py:77
  54.5 129.8 %all-gather.5.cloned.1.call-start = ((), (), s32[]{:S(2)}) async-start(), calls=%async_computation.5 | async-start | bytes 9437184 | tf_op jit(solution)/shard_map/all_gather | solution.py:94
  81.8 16.3 %copy-start.7 = (bf16[8,64,1024]{2,1,0:T(8,128)(2,1)S(1)}, bf16[8,64,1024]{2,1,0:T(8,128)(2,1)}, u32[]{:S(2)}) copy-start(bf16[8,64,1024]{2,1,0:T(8,128)(2,1)} %param.13) | copy-start | bytes 3145732
  98.1 1.8 copy-start.9
  98.1 1.8 copy-start.12
  98.1 1.8 copy-start.13
  99.5 6.9 %copy-start.3 = (bf16[8,64,1024]{2,1,0:T(8,128)(2,1)}, bf16[8,64,1024]{2,1,0:T(8,128)(2,1)S(1)}, u32[]{:S(2)}) copy-start(bf16[8,64,1024]{2,1,0:T(8,128)(2,1)S(1)} %get-tuple-element.8) | copy-start | bytes 3145732
  102.3 164.1 %all-gather.3.cloned.1.call-start = ((), (), s32[]{:S(2)}) async-start(), calls=%async_computation.4 | async-start | bytes 9437184 | tf_op jit(solution)/shard_map/all_gather | solution.py:95
  200.8 5.7 %copy-start.2 = (f32[8,16,64,512]{3,2,1,0:T(8,128)}, f32[8,16,64,512]{3,2,1,0:T(8,128)S(1)}, u32[]{:S(2)}) copy-start(f32[8,16,64,512]{3,2,1,0:T(8,128)S(1)} %get-tuple-element.10) | copy-start | bytes 50331652
  277.9 10.2 %copy-start.4 = (bf16[8,64,1024]{2,1,0:T(8,128)(2,1)S(1)}, bf16[8,64,1024]{2,1,0:T(8,128)(2,1)}, u32[]{:S(2)}) copy-start(bf16[8,64,1024]{2,1,0:T(8,128)(2,1)} %copy-done.3) | copy-start | bytes 3145732
  277.9 10.2 %copy-start.8 = (bf16[1024,1024]{1,0:T(8,128)(2,1)S(1)}, bf16[1024,1024]{1,0:T(8,128)(2,1)}, u32[]{:S(2)}) copy-start(bf16[1024,1024]{1,0:T(8,128)(2,1)} %param.25) | copy-start | bytes 6291460
  288.1 2.3 copy-start.1
Sparse Core Ops, SparseCore 0:
  102.5 81.7 all-gather.4
  185.9 80.5 all-gather.2
where the time goes:
time: 298 us; the launch traced here: 297 us
  waiting for transfers between devices  143 us (48%)
  local copies, waits for them, and re-layouts  51.9 us (17%)
  matrix products  47.8 us (16%)
  blocking collectives  16.2 us (5%)
  between operations  13.7 us (5%)
  starting transfers between devices  13.2 us (4%)
  other arithmetic  11 us (4%)
    all_gather x1, waiting for transfers between devices, body(): lax.all_gather(space_keys, 'space', axis=1, tiled=True)  71.1 us
    all_gather x1, waiting for transfers between devices, body(): lax.all_gather(space_values, 'space', axis=1, tiled=True)  55.7 us
    dot_general x8, matrix products, project(): return jnp.dot(tokens, weight, preferred_element_type=jnp.float32)  23.2 us
    all_to_all x1, blocking collectives, body(): lax.all_to_all(attended, 'tm', split_axis=0, concat_axis=1, tiled=True)  16.2 us
    all_gather x1, local copies, waits for them, and re-layouts, body(): lax.all_gather(space_keys, 'space', axis=1, tiled=True)  11.7 us
    all_gather x1, local copies, waits for them, and re-layouts, body(): lax.all_gather(space_values, 'space', axis=1, tiled=True)  11.4 us
    another operation x3, local copies, waits for them, and re-layouts, split_heads(): tokens.reshape(tokens.shape[0], tokens.shape[1], tokens.shape[2] // HEAD_...  10.4 us
    dot_general x1, matrix products, body(): jnp.einsum('fhqk,fkhd->fqhd', weights.astype(jnp.bfloat16), split_heads(p...  10.2 us
  transfers between devices with their start and end apart: 5, of which 5 were waited for; matrix products, arithmetic and copies ran while one was open for 18% of the time, Pallas kernels for 0%

commit v1 on v0

v1 whole, which is shorter than its diff:
```python
import functools
import math

import jax
import jax.numpy as jnp
from jax import lax
from jax.experimental import pallas as pl
from jax.experimental.pallas import tpu as pltpu
from jax.sharding import PartitionSpec as P

HEAD_DIM = 64
LANES = 128
SCALE = 0.125 * math.log2(math.e)
F32, BF16 = jnp.float32, jnp.bfloat16


def layer_norm(tokens, gain, shift):
    values = tokens.astype(F32)
    mean_value = jnp.mean(values, axis=-1, keepdims=True)
    centred = values - mean_value
    variance = jnp.mean(centred * centred, axis=-1, keepdims=True)
    return (centred * lax.rsqrt(variance + 1e-05) * gain + shift).astype(BF16)


def project(tokens, weight):
    return jnp.dot(tokens, weight, preferred_element_type=F32)


def permutation(rows, inner, outer, back):
    row = lax.broadcasted_iota(jnp.int32, (rows, rows), 1 if back else 0)
    col = lax.broadcasted_iota(jnp.int32, (rows, rows), 0 if back else 1)
    return jnp.where((row % inner) * outer + row // inner == col, 1.0, 0.0).astype(BF16)


def lane_masks(width):
    lane = lax.broadcasted_iota(jnp.int32, (1, LANES), 1)
    return [(lane // HEAD_DIM == part) for part in range(LANES // HEAD_DIM)]


def attend(queries, keys_in, values_in, same):
    result = None
    for mask in lane_masks(LANES):
        own = jnp.where(mask, queries, jnp.zeros_like(queries))
        scores = lax.dot_general(
            own, keys_in, (((1,), (1,)), ((), ())), preferred_element_type=F32
        )
        if same is not None:
            scores = jnp.where(same, scores, -1e30)
        top = jnp.max(scores, axis=-1, keepdims=True)
        weights = jnp.exp2((scores - top) * SCALE)
        total = jnp.sum(weights, axis=-1, keepdims=True)
        added = jnp.dot(weights.astype(BF16), values_in, preferred_element_type=F32) / total
        result = added if result is None else jnp.where(mask, added, result)
    return result.astype(BF16)


def qkv(normed, weights, waits, outs):
    for weight, wait, out in zip(weights, waits, outs):
        wait()
        out[...] = project(normed, weight[...]).astype(BF16)


def time_branch(frames, x, gain, shift, weights, waits, q, k, v, a):
    rows, width = q.shape
    places = rows // frames
    order = permutation(rows, frames, places, False)
    x = project(order, x).astype(BF16)
    qkv(layer_norm(x, gain, shift), weights[:3], waits[:3], (q, k, v))
    size = max(frames, LANES)
    same = (
        lax.broadcasted_iota(jnp.int32, (size, size), 0) // frames
        == lax.broadcasted_iota(jnp.int32, (size, size), 1) // frames
    )

    def pair(index, carry):
        cols = pl.ds(pl.multiple_of(index * LANES, LANES), LANES)
        for group in range(rows // size):
            part = (pl.ds(group * size, size), cols)
            a[part] = attend(q[part], k[part], v[part], same)
        return carry

    lax.fori_loop(0, width // LANES, pair, 0)
    waits[3]()
    after = (x.astype(F32) + project(a[...], weights[3][...])).astype(BF16)
    return project(permutation(rows, frames, places, True), after).astype(BF16)


def space_branch(x, gain, shift, weights, waits, q, k, v, a):
    rows, width = q.shape
    qkv(layer_norm(x, gain, shift), weights[:3], waits[:3], (q, k, v))

    def pair(index, carry):
        cols = pl.ds(pl.multiple_of(index * LANES, LANES), LANES)
        a[:, cols] = attend(q[:, cols], k[:, cols], v[:, cols], None)
        return carry

    lax.fori_loop(0, width // LANES, pair, 0)
    waits[3]()
    return (x.astype(F32) + project(a[...], weights[3][...])).astype(BF16)


def branch_kernel(branch, x, gain, shift, w0, w1, w2, w3, out, held, q, k, v, a, sems):
    copies = [
        pltpu.make_async_copy(w, held.at[i], sems.at[i]) for i, w in enumerate((w0, w1, w2, w3))
    ]
    for copy in copies:
        copy.start()
    weights = [held.at[i] for i in range(4)]
    waits = [copy.wait for copy in copies]
    out[...] = branch(x[...], gain[...], shift[...], weights, waits, q, k, v, a)


def run_branch(branch, x, gain, shift, *weights):
    rows, width = x.shape
    vmem = pl.BlockSpec(memory_space=pltpu.VMEM)
    return pl.pallas_call(
        functools.partial(branch_kernel, branch),
        out_shape=jax.ShapeDtypeStruct((rows, width), BF16),
        in_specs=[vmem] * 3 + [pl.BlockSpec(memory_space=pl.ANY)] * 4,
        out_specs=vmem,
        scratch_shapes=[pltpu.VMEM((4, width, width), BF16)]
        + [pltpu.VMEM((rows, width), BF16)] * 4
        + [pltpu.SemaphoreType.DMA((4,))],
        compiler_params=pltpu.CompilerParams(vmem_limit_bytes=60 << 20),
    )(x, gain.reshape(1, -1), shift.reshape(1, -1), *weights)


def split_heads(tokens):
    return tokens.reshape(tokens.shape[0], tokens.shape[1], tokens.shape[2] // HEAD_DIM, HEAD_DIM)


def gathered_space(after_time, gain, shift, wq, wk, wv, wo):
    normed = layer_norm(after_time, gain, shift)
    queries = project(normed, wq).astype(BF16)
    everywhere = lax.all_gather(normed, "space", axis=1, tiled=True)
    keys_in, values_in = (project(everywhere, w).astype(BF16) for w in (wk, wv))
    scores = 0.125 * jnp.einsum(
        "fqhd,fkhd->fhqk", split_heads(queries), split_heads(keys_in), preferred_element_type=F32
    )
    weights = jax.nn.softmax(scores, axis=-1).astype(BF16)
    spatial = jnp.einsum(
        "fhqk,fkhd->fqhd", weights, split_heads(values_in), preferred_element_type=F32
    )
    spatial = spatial.astype(BF16).reshape(after_time.shape)
    return (after_time.astype(F32) + project(spatial, wo)).astype(BF16)


def body(frames_in, tg, ts, tq, tk, tv, to, sg, ss, sq, sk, sv, so):
    slots, spread = lax.axis_size("tm"), lax.axis_size("space")
    rows, patches, width = frames_in.shape
    frames, places = rows * slots, patches // slots
    tokens = lax.all_to_all(
        frames_in.reshape(rows, slots, places, width), "tm", split_axis=1, concat_axis=0, tiled=True
    ).reshape(frames * places, width)
    after = run_branch(functools.partial(time_branch, frames), tokens, tg, ts, tq, tk, tv, to)
    if rows != spread:
        after = lax.all_to_all(
            after.reshape(frames, 1, places, width), "tm", split_axis=0, concat_axis=1, tiled=True
        ).reshape(rows, patches, width)
        return gathered_space(after, sg, ss, sq, sk, sv, so)
    frame = lax.all_to_all(
        after.reshape(frames, places, width), ("tm", "space"), split_axis=0, concat_axis=0, tiled=True
    ).reshape(frames * places, width)
    done = run_branch(space_branch, frame, sg, ss, sq, sk, sv, so)
    done = done.reshape(slots, spread, places, width).transpose(1, 0, 2, 3)
    return lax.all_to_all(done, "space", split_axis=0, concat_axis=0, tiled=True).reshape(
        rows, patches, width
    )


def solution(mesh):
    return jax.shard_map(
        body,
        mesh=mesh,
        in_specs=(P("tm", "space", None),) + (P(),) * 12,
        out_specs=P("tm", "space", None),
        check_vma=False,
    )
```

time: 298 us -> 127 us (0.43)
  waiting for transfers between devices: 143 us -> 0 us
  blocking collectives: 16.2 us -> 80.1 us
  local copies, waits for them, and re-layouts: 51.9 us -> 3.57 us
  matrix products: 47.8 us -> 0 us
  Pallas kernels: 0 us -> 43.2 us
  between operations: 13.7 us -> 0.03 us
  starting transfers between devices: 13.2 us -> 0 us
  other arithmetic: 11 us -> 0 us
    all_gather x2 -> x0, waiting for transfers between devices: 127 us -> none  [the longest x1 71.1 us: body(): lax.all_gather(space_keys, 'space', axis=1, tiled=True)]
    all_to_all x1 -> x3, blocking collectives: 16.2 us -> 80.1 us  [the longest x1 31.9 us: body(): lax.all_to_all(after.reshape(frames, places, width), ('tm', 'space'), spl...]
    dot_general x12 -> x0, matrix products: 47.8 us -> none  [the longest x8 23.2 us: project(): return jnp.dot(tokens, weight, preferred_element_type=jnp.float32)]
    pallas_call x0 -> x2, Pallas kernels: none -> 43.2 us  [run_branch(): pl.pallas_call(functools.partial(branch_kernel, branch), out_shape=jax.Sh...]
    all_gather x2 -> x0, local copies, waits for them, and re-layouts: 23.1 us -> none  [the longest x1 11.7 us: body(): lax.all_gather(space_keys, 'space', axis=1, tiled=True)]
    all_to_all x3 -> x0, waiting for transfers between devices: 16.7 us -> none  [the longest x1 9.35 us: body(): lax.all_to_all(projected[0], 'tm', split_axis=1, concat_axis=0, tiled=True)]
    another operation x4 -> x0, local copies, waits for them, and re-layouts: 13.6 us -> none  [the longest x3 10.4 us: split_heads(): tokens.reshape(tokens.shape[0], tokens.shape[1], tokens.shape[2] // HEAD_...]
    all_to_all x3 -> x0, starting transfers between devices: 12.9 us -> none  [the longest x1 5.18 us: body(): lax.all_to_all(projected[0], 'tm', split_axis=1, concat_axis=0, tiled=True)]
  transfers between devices with their start and end apart: 5 -> 0, of which waited for: 5 -> 0; matrix products, arithmetic and copies ran while one was open for 18% -> 0% of each run, Pallas kernels for 0% -> 0%
where the time goes in v1:
time: 127 us
  blocking collectives  80.1 us (63%)
  Pallas kernels  43.2 us (34%)
  local copies, waits for them, and re-layouts  3.57 us (3%)
    pallas_call x2, Pallas kernels, run_branch(): pl.pallas_call(functools.partial(branch_kernel, branch), out_shape=jax.Sh...  43.2 us
    all_to_all x1, blocking collectives, body(): lax.all_to_all(after.reshape(frames, places, width), ('tm', 'space'), spl...  31.9 us
    all_to_all x1, blocking collectives, body(): lax.all_to_all(done, 'space', split_axis=0, concat_axis=0, tiled=True)  29 us
    all_to_all x1, blocking collectives, body(): lax.all_to_all(frames_in.reshape(rows, slots, places, width), 'tm', split...  19.2 us

profile of v1, /device:TPU:0, one launch (start us, length us, event | category | flops | bytes accessed | tf_op | source)
XLA Modules:
  0.0 126.9 jit_solution(266573444348871420)
XLA Ops:
  0.0 1.3 %copy.16 = bf16[8,4,16,1024]{3,2,0,1:T(8,128)(2,1)S(1)} copy(bf16[8,4,16,1024]{3,2,1,0:T(8,128)(2,1)} %bitcast.23) | data formatting | bytes 2097152 | tf_op jit(solution)/shard_map/reshape | solution.py:153
  1.3 19.2 %all_to_all.25 = bf16[8,4,16,1024]{3,2,0,1:T(8,128)(2,1)} all-to-all(bf16[8,4,16,1024]{3,2,0,1:T(8,128)(2,1)S(1)} %copy.16), channel_id=1, replica_groups=mesh['tm'=4,'space'=8] {'tm'}, dimensions={1} | all-to-all | bytes 2097152 | tf_op jit(solution)/shard_map/all_to_all | solution.py:152
  20.5 25.6 %shard_map.127 = bf16[512,1024]{1,0:T(8,128)(2,1)} custom-call(bf16[512,1024]{1,0:T(8,128)(2,1)} %bitcast.17, f32[1,1024]{1,0:T(1,128)} %bitcast.24, f32[1,1024]{1,0:T(1,128)} %bitcast.25, bf16[1024,1024]{1,0:T(8,128)(2,1)} %w0.2, bf16[1024,1024]{1,0:T(8,128)(2,1)} %w1.2, bf16[1024,1024]{1,0:T(8,128)(2,1)} %w2.2, bf16[1024,1024]{1,0:T(8,128)(2,1)} %w3.2), custom_call_target="tpu_custom_call" | custom-call | tf_op jit(solution)/shard_map/pallas_call | solution.py:116
  46.2 31.9 %all_to_all.26 = bf16[32,16,1024]{2,1,0:T(8,128)(2,1)} all-to-all(bf16[32,16,1024]{2,1,0:T(8,128)(2,1)} %bitcast.18), channel_id=1, replica_groups=mesh['tm'=4,'space'=8] {'tm','space'}, dimensions={0} | all-to-all | bytes 2097152 | tf_op jit(solution)/shard_map/all_to_all | solution.py:161
  78.1 17.5 %shard_map.128 = bf16[512,1024]{1,0:T(8,128)(2,1)} custom-call(bf16[512,1024]{1,0:T(8,128)(2,1)} %bitcast.19, f32[1,1024]{1,0:T(1,128)} %bitcast.26, f32[1,1024]{1,0:T(1,128)} %bitcast.27, bf16[1024,1024]{1,0:T(8,128)(2,1)} %w0.3, bf16[1024,1024]{1,0:T(8,128)(2,1)} %w1.3, bf16[1024,1024]{1,0:T(8,128)(2,1)} %w2.3, bf16[1024,1024]{1,0:T(8,128)(2,1)} %w3.3), custom_call_target="tpu_custom_call" | custom-call | tf_op jit(solution)/shard_map/pallas_call | solution.py:116
  95.6 1.3 %copy.19 = bf16[4,8,16,1024]{3,2,0,1:T(8,128)(2,1)S(1)} copy(bf16[4,8,16,1024]{3,2,1,0:T(8,128)(2,1)} %bitcast.20) | data formatting | bytes 2097152 | tf_op jit(solution)/shard_map/reshape | solution.py:165
  96.9 29.0 %all_to_all.27 = bf16[8,4,16,1024]{3,2,1,0:T(8,128)(2,1)S(1)} all-to-all(bf16[8,4,16,1024]{3,2,1,0:T(8,128)(2,1)S(1)} %bitcast.21), channel_id=1, replica_groups=mesh['tm'=4,'space'=8] {'space'}, dimensions={0} | all-to-all | bytes 2097152 | tf_op jit(solution)/shard_map/all_to_all | solution.py:166
  125.9 1.0 copy.21

commit v2 on v1

--- a/solution.py
+++ b/solution.py
@@ -38,19 +38,20 @@
 
 
 def attend(queries, keys_in, values_in, same):
-    result = None
-    for mask in lane_masks(LANES):
-        own = jnp.where(mask, queries, jnp.zeros_like(queries))
-        scores = lax.dot_general(
-            own, keys_in, (((1,), (1,)), ((), ())), preferred_element_type=F32
-        )
-        if same is not None:
-            scores = jnp.where(same, scores, -1e30)
-        top = jnp.max(scores, axis=-1, keepdims=True)
-        weights = jnp.exp2((scores - top) * SCALE)
-        total = jnp.sum(weights, axis=-1, keepdims=True)
-        added = jnp.dot(weights.astype(BF16), values_in, preferred_element_type=F32) / total
-        result = added if result is None else jnp.where(mask, added, result)
+    rows = queries.shape[0]
+    masks = lane_masks(LANES)
+    own = jnp.concatenate([jnp.where(mask, queries, jnp.zeros_like(queries)) for mask in masks], 0)
+    scores = lax.dot_general(own, keys_in, (((1,), (1,)), ((), ())), preferred_element_type=F32)
+    if same is not None:
+        scores = jnp.where(jnp.concatenate([same] * len(masks), 0), scores, -1e30)
+    top = jnp.max(scores, axis=-1, keepdims=True)
+    weights = jnp.exp2((scores - top) * SCALE).astype(BF16)
+    both = jnp.concatenate([values_in, jnp.ones_like(values_in)], 1)
+    added = jnp.dot(weights, both, preferred_element_type=F32)
+    added = added[:, :LANES] / added[:, LANES:]
+    result = added[:rows]
+    for part in range(1, len(masks)):
+        result = jnp.where(masks[part], added[part * rows : (part + 1) * rows], result)
     return result.astype(BF16)
 
 
@@ -79,24 +80,10 @@
             a[part] = attend(q[part], k[part], v[part], same)
         return carry
 
-    lax.fori_loop(0, width // LANES, pair, 0)
+    lax.fori_loop(0, width // LANES, pair, 0, unroll=2)
     waits[3]()
     after = (x.astype(F32) + project(a[...], weights[3][...])).astype(BF16)
-    return project(permutation(rows, frames, places, True), after).astype(BF16)
-
-
-def space_branch(x, gain, shift, weights, waits, q, k, v, a):
-    rows, width = q.shape
-    qkv(layer_norm(x, gain, shift), weights[:3], waits[:3], (q, k, v))
-
-    def pair(index, carry):
-        cols = pl.ds(pl.multiple_of(index * LANES, LANES), LANES)
-        a[:, cols] = attend(q[:, cols], k[:, cols], v[:, cols], None)
-        return carry
-
-    lax.fori_loop(0, width // LANES, pair, 0)
-    waits[3]()
-    return (x.astype(F32) + project(a[...], weights[3][...])).astype(BF16)
+    return project(permutation(rows, frames, places, True), after)
 
 
 def branch_kernel(branch, x, gain, shift, w0, w1, w2, w3, out, held, q, k, v, a, sems):
@@ -107,7 +94,7 @@
         copy.start()
     weights = [held.at[i] for i in range(4)]
     waits = [copy.wait for copy in copies]
-    out[...] = branch(x[...], gain[...], shift[...], weights, waits, q, k, v, a)
+    out[...] = branch(x[...], gain[...], shift[...], weights, waits, q, k, v, a).astype(BF16)
 
 
 def run_branch(branch, x, gain, shift, *weights):
@@ -125,6 +112,201 @@
     )(x, gain.reshape(1, -1), shift.reshape(1, -1), *weights)
 
 
+def flipped(index, mask):
+    result, bit = index + mask, 1
+    while bit < 64:
+        result = result - 2 * bit * ((index // bit) % 2) * ((mask // bit) % 2)
+        bit *= 2
+    return result
+
+
+def layer_kernel(
+    slots,
+    spread,
+    x,
+    tg,
+    ts,
+    sg,
+    ss,
+    *refs,
+):
+    sources, out = refs[:8], refs[8]
+    held, xt, snd, rcv, done, q, k, v, a, wsem, lsem, s1, r1, s2, r2, s3, r3 = refs[9:]
+    me_t, me_s = lax.axis_index("tm"), lax.axis_index("space")
+    frames, piece, width = xt.shape[1:]
+    rows, halves = frames // slots, xt.shape[0]
+    peers = slots * spread
+    tokens = frames * piece
+
+    def device(mask):
+        return flipped(me_t, mask % slots), flipped(me_s, mask // slots)
+
+    barrier = pltpu.get_barrier_semaphore()
+
+    def greet(n, carry):
+        t, s = device(n + 1)
+        pl.semaphore_signal(barrier, inc=1, device_id={"tm": t, "space": s})
+        return carry
+
+    lax.fori_loop(0, peers - 1, greet, 0)
+    loads = [pltpu.make_async_copy(w, held.at[i], wsem.at[i]) for i, w in enumerate(sources)]
+    locals_in = [
+        pltpu.make_async_copy(
+            x.at[:, me_t, h], xt.at[h, pl.ds(me_t * rows, rows)], lsem.at[h]
+        )
+        for h in range(halves)
+    ]
+    for copy in locals_in + loads:
+        copy.start()
+    pl.semaphore_wait(barrier, peers - 1)
+
+    def first(h, mask):
+        t = flipped(me_t, mask)
+        return pltpu.make_async_remote_copy(
+            src_ref=x.at[:, t, h],
+            dst_ref=xt.at[h, pl.ds(me_t * rows, rows)],
+            send_sem=s1.at[h, mask],
+            recv_sem=r1.at[h, mask],
+            device_id={"tm": t},
+        )
+
+    def second(h, mask):
+        t, s = device(mask)
+        return pltpu.make_async_remote_copy(
+            src_ref=snd.at[h, t * rows + s],
+            dst_ref=rcv.at[(me_s * slots + me_t) * halves + h],
+            send_sem=s2.at[h, mask],
+            recv_sem=r2.at[h, mask],
+            device_id={"tm": t, "space": s},
+        )
+
+    for h in range(halves):
+        for mask in range(slots - 1, 0, -1):
+            first(h, mask).start()
+
+    weights = [held.at[i] for i in range(8)]
+    waits = [copy.wait for copy in loads]
+    for h in range(halves):
+        locals_in[h].wait()
+        for mask in range(1, slots):
+            first(h, mask).wait_recv()
+        part = [ref.at[pl.ds(0, tokens)] for ref in (q, k, v, a)]
+        after = time_branch(
+            frames,
+            xt[h].astype(F32).reshape(tokens, width).astype(BF16),
+            tg[...],
+            ts[...],
+            weights[:4],
+            waits[:4] if h == 0 else [lambda: None] * 4,
+            *part,
+        )
+        after = after.reshape(frames, piece, width).astype(BF16)
+        snd[h] = after
+
+        def send(n, carry):
+            second(h, peers - 1 - n).start()
+            return carry
+
+        lax.fori_loop(0, peers - 1, send, 0)
+        rcv[(me_s * slots + me_t) * halves + h] = snd[h, me_t * rows + me_s]
+
+    def arrive(n, carry):
+        for h in range(halves):
+            second(h, peers - 1 - n).wait_recv()
+        return carry
+
+    lax.fori_loop(0, peers - 1, arrive, 0)
+    total = q.shape[0]
+    frame = rcv[...].astype(F32).reshape(total, width).astype(BF16)
+    done[...] = frame
+    qkv(layer_norm(frame, sg[...], ss[...]), weights[4:7], waits[4:7], (q, k, v))
+    waits[7]()
+    share = total // spread
+    group = 2 if spread % 2 == 0 else 1
+    steps = spread // group
+
+    def third(mask):
+        s = flipped(me_s, mask)
+        return pltpu.make_async_remote_copy(
+            src_ref=done.at[pl.ds(pl.multiple_of(s * share, share), share)],
+            dst_ref=out.at[me_s],
+            send_sem=s3.at[mask],
+            recv_sem=r3.at[mask],
+            device_id={"space": s},
+        )
+
+    for step in range(steps - 1, -1, -1):
+        size = group * share
+        chunk = pl.ds(pl.multiple_of(flipped(me_s // group, step) * size, size), size)
+
+        def pair(index, carry):
+            cols = pl.ds(pl.multiple_of(index * LANES, LANES), LANES)
+            a[chunk, cols] = attend(q[chunk, cols], k[:, cols], v[:, cols], None)
+            return carry
+
+        lax.fori_loop(0, width // LANES, pair, 0, unroll=2)
+        done[chunk] = (done[chunk].astype(F32) + project(a[chunk], weights[7][...])).astype(BF16)
+        for member in range(group - 1, -1, -1):
+            if step * group + member:
+                third(step * group + member).start()
+    last = pltpu.make_async_copy(
+        done.at[pl.ds(pl.multiple_of(me_s * share, share), share)], out.at[me_s], lsem.at[0]
+    )
+    last.start()
+    for h in range(halves):
+        for mask in range(1, slots):
+            first(h, mask).wait_send()
+
+    def left(n, carry):
+        for h in range(halves):
+            second(h, n + 1).wait_send()
+        return carry
+
+    lax.fori_loop(0, peers - 1, left, 0)
+    for mask in range(1, spread):
+        third(mask).wait()
+    last.wait()
+
+
+def run_layer(frames_in, slots, spread, norms, weights):
+    rows, patches, width = frames_in.shape
+    frames, places, halves = rows * slots, patches // slots, 2
+    piece = places // halves
+    total = frames * places
+    vmem, hbm = pl.BlockSpec(memory_space=pltpu.VMEM), pl.BlockSpec(memory_space=pl.ANY)
+    dma = pltpu.SemaphoreType.DMA
+    return pl.pallas_call(
+        functools.partial(layer_kernel, slots, spread),
+        out_shape=jax.ShapeDtypeStruct(frames_in.shape, BF16),
+        in_specs=[hbm] + [vmem] * 4 + [hbm] * 8,
+        out_specs=hbm,
+        scratch_shapes=[
+            pltpu.VMEM((8, width, width), BF16),
+            pltpu.VMEM((halves, frames, piece, width), BF16),
+            pltpu.VMEM((halves, frames, piece, width), BF16),
+            pltpu.VMEM((total // piece, piece, width), BF16),
+        ]
+        + [pltpu.VMEM((total, width), BF16)] * 5
+        + [
+            dma((8,)),
+            dma((halves,)),
+            dma((halves, slots)),
+            dma((halves, slots)),
+            dma((halves, slots * spread)),
+            dma((halves, slots * spread)),
+            dma((spread,)),
+            dma((spread,)),
+        ],
+        compiler_params=pltpu.CompilerParams(
+            collective_id=0, has_side_effects=True, vmem_limit_bytes=60 << 20
+        ),
+    )(
+        frames_in.reshape(rows, slots, halves, piece, width),
+        *[norm.reshape(1, -1) for norm in norms],
+        *weights,
+    )
+
+
 def split_heads(tokens):
     return tokens.reshape(tokens.shape[0], tokens.shape[1], tokens.shape[2] // HEAD_DIM, HEAD_DIM)
 
@@ -149,23 +331,18 @@
     slots, spread = lax.axis_size("tm"), lax.axis_size("space")
     rows, patches, width = frames_in.shape
     frames, places = rows * slots, patches // slots
+    if rows == spread and not (slots & (slots - 1) or spread & (spread - 1)):
+        return run_layer(
+            frames_in, slots, spread, (tg, ts, sg, ss), (tq, tk, tv, to, sq, sk, sv, so)
+        )
     tokens = lax.all_to_all(
         frames_in.reshape(rows, slots, places, width), "tm", split_axis=1, concat_axis=0, tiled=True
     ).reshape(frames * places, width)
     after = run_branch(functools.partial(time_branch, frames), tokens, tg, ts, tq, tk, tv, to)
-    if rows != spread:
-        after = lax.all_to_all(
-            after.reshape(frames, 1, places, width), "tm", split_axis=0, concat_axis=1, tiled=True
-        ).reshape(rows, patches, width)
-        return gathered_space(after, sg, ss, sq, sk, sv, so)
-    frame = lax.all_to_all(
-        after.reshape(frames, places, width), ("tm", "space"), split_axis=0, concat_axis=0, tiled=True
-    ).reshape(frames * places, width)
-    done = run_branch(space_branch, frame, sg, ss, sq, sk, sv, so)
-    done = done.reshape(slots, spread, places, width).transpose(1, 0, 2, 3)
-    return lax.all_to_all(done, "space", split_axis=0, concat_axis=0, tiled=True).reshape(
-        rows, patches, width
-    )
+    after = lax.all_to_all(
+        after.reshape(frames, 1, places, width), "tm", split_axis=0, concat_axis=1, tiled=True
+    ).reshape(rows, patches, width)
+    return gathered_space(after, sg, ss, sq, sk, sv, so)
 
 
 def solution(mesh):

time: 127 us -> 82.9 us (0.65)
  blocking collectives: 80.1 us -> 0 us
  Pallas kernels: 43.2 us -> 80.4 us
  local copies, waits for them, and re-layouts: 3.57 us -> 2.26 us
    all_to_all x3 -> x0, blocking collectives: 80.1 us -> none  [the longest x1 31.9 us: body(): lax.all_to_all(after.reshape(frames, places, width), ('tm', 'space'), spl...]
    pallas_call x2 -> x1, Pallas kernels: 43.2 us -> 80.4 us  [run_layer(): pl.pallas_call(functools.partial(layer_kernel, slots, spread), out_shape=...]
    reshape x2 -> x0, local copies, waits for them, and re-layouts: 2.6 us -> none  [the longest x1 1.3 us: body(): done = done.reshape(slots, spread, places, width).transpose(1, 0, 2, 3)]
    unnamed x1, local copies, waits for them, and re-layouts: 0.97 us -> 2.26 us
where the time goes in v2:
time: 82.9 us; the launch traced here: 82.7 us
  Pallas kernels  80.4 us (97%)
  local copies, waits for them, and re-layouts  2.26 us (3%)
    pallas_call x1, Pallas kernels, run_layer(): pl.pallas_call(functools.partial(layer_kernel, slots, spread), out_shape=...  80.4 us
    unnamed x1, local copies, waits for them, and re-layouts  2.26 us

profile of v2, /device:TPU:0, one launch (start us, length us, event | category | flops | bytes accessed | tf_op | source)
XLA Modules:
  0.0 82.7 jit_solution(15719102772082685276)
XLA Ops:
  0.0 80.4 %shard_map.127 = bf16[8,64,1024]{2,1,0:T(8,128)(2,1)} custom-call(bf16[8,4,2,8,1024]{4,3,2,1,0:T(8,128)(2,1)} %bitcast.5, f32[1,1024]{1,0:T(1,128)} %bitcast.6, f32[1,1024]{1,0:T(1,128)} %bitcast.7, f32[1,1024]{1,0:T(1,128)} %bitcast.8, f32[1,1024]{1,0:T(1,128)} %bitcast.9, bf16[1024,1024]{1,0:T(8,128)(2,1)} %refs_0_.1, bf16[1024,1024]{1,0:T(8,128)(2,1)} %refs_1_.1, ...), custom_call_target="tpu_custom_call" | custom-call | tf_op jit(solution)/shard_map/pallas_call | solution.py:278
  80.5 2.3 %copy.15 = bf16[8,64,1024]{2,1,0:T(8,128)(2,1)} copy(bf16[8,64,1024]{2,1,0:T(8,128)(2,1)} %shard_map.127) | data formatting | bytes 2097152

commit v3 on v2

--- a/solution.py
+++ b/solution.py
@@ -131,7 +131,7 @@
     *refs,
 ):
     sources, out = refs[:8], refs[8]
-    held, xt, snd, rcv, done, q, k, v, a, wsem, lsem, s1, r1, s2, r2, s3, r3 = refs[9:]
+    held, xt, snd, rcv, q, k, v, a, wsem, lsem, s1, r1, s2, r2, s3, r3 = refs[9:]
     me_t, me_s = lax.axis_index("tm"), lax.axis_index("space")
     frames, piece, width = xt.shape[1:]
     rows, halves = frames // slots, xt.shape[0]
@@ -174,7 +174,7 @@
         t, s = device(mask)
         return pltpu.make_async_remote_copy(
             src_ref=snd.at[h, t * rows + s],
-            dst_ref=rcv.at[(me_s * slots + me_t) * halves + h],
+            dst_ref=rcv.at[h * peers + me_s * slots + me_t],
             send_sem=s2.at[h, mask],
             recv_sem=r2.at[h, mask],
             device_id={"tm": t, "space": s},
@@ -208,51 +208,71 @@
             return carry
 
         lax.fori_loop(0, peers - 1, send, 0)
-        rcv[(me_s * slots + me_t) * halves + h] = snd[h, me_t * rows + me_s]
-
-    def arrive(n, carry):
-        for h in range(halves):
+        rcv[h * peers + me_s * slots + me_t] = snd[h, me_t * rows + me_s]
+
+    for h in range(halves):
+
+        def arrive(n, carry):
             second(h, peers - 1 - n).wait_recv()
-        return carry
-
-    lax.fori_loop(0, peers - 1, arrive, 0)
-    total = q.shape[0]
-    frame = rcv[...].astype(F32).reshape(total, width).astype(BF16)
-    done[...] = frame
-    qkv(layer_norm(frame, sg[...], ss[...]), weights[4:7], waits[4:7], (q, k, v))
+            return carry
+
+        lax.fori_loop(0, peers - 1, arrive, 0)
+        frame = rcv[pl.ds(h * peers, peers)].astype(F32).reshape(tokens, width).astype(BF16)
+        qkv(
+            layer_norm(frame, sg[...], ss[...]),
+            weights[4:7],
+            waits[4:7] if h == 0 else [lambda: None] * 3,
+            [ref.at[pl.ds(h * tokens, tokens)] for ref in (q, k, v)],
+        )
     waits[7]()
-    share = total // spread
+    share = slots * piece
     group = 2 if spread % 2 == 0 else 1
     steps = spread // group
 
-    def third(mask):
+    def blocks(h, s, count):
+        return pl.ds(h * peers + s * slots, count * slots)
+
+    def third(h, mask):
         s = flipped(me_s, mask)
         return pltpu.make_async_remote_copy(
-            src_ref=done.at[pl.ds(pl.multiple_of(s * share, share), share)],
-            dst_ref=out.at[me_s],
-            send_sem=s3.at[mask],
-            recv_sem=r3.at[mask],
+            src_ref=rcv.at[blocks(h, s, 1)],
+            dst_ref=out.at[me_s, :, h],
+            send_sem=s3.at[h, mask],
+            recv_sem=r3.at[h, mask],
             device_id={"space": s},
         )
 
     for step in range(steps - 1, -1, -1):
         size = group * share
-        chunk = pl.ds(pl.multiple_of(flipped(me_s // group, step) * size, size), size)
+        base = flipped(me_s // group, step) * group
+        parts = [
+            pl.ds(pl.multiple_of(h * tokens + base * share, size), size) for h in range(halves)
+        ]
 
         def pair(index, carry):
             cols = pl.ds(pl.multiple_of(index * LANES, LANES), LANES)
-            a[chunk, cols] = attend(q[chunk, cols], k[:, cols], v[:, cols], None)
+            queries = jnp.concatenate([q[part, cols] for part in parts], 0)
+            result = attend(queries, k[:, cols], v[:, cols], None)
+            for h, part in enumerate(parts):
+                a[part, cols] = result[h * size : (h + 1) * size]
             return carry
 
         lax.fori_loop(0, width // LANES, pair, 0, unroll=2)
-        done[chunk] = (done[chunk].astype(F32) + project(a[chunk], weights[7][...])).astype(BF16)
+        added = project(jnp.concatenate([a[part] for part in parts], 0), weights[7][...])
+        for h in range(halves):
+            here = blocks(h, base, group)
+            new = added[h * size : (h + 1) * size].reshape(group * slots, piece, width)
+            rcv[here] = (rcv[here].astype(F32) + new).astype(BF16)
         for member in range(group - 1, -1, -1):
             if step * group + member:
-                third(step * group + member).start()
-    last = pltpu.make_async_copy(
-        done.at[pl.ds(pl.multiple_of(me_s * share, share), share)], out.at[me_s], lsem.at[0]
-    )
-    last.start()
+                for h in range(halves):
+                    third(h, step * group + member).start()
+    last = [
+        pltpu.make_async_copy(rcv.at[blocks(h, me_s, 1)], out.at[me_s, :, h], lsem.at[h])
+        for h in range(halves)
+    ]
+    for copy in last:
+        copy.start()
     for h in range(halves):
         for mask in range(1, slots):
             first(h, mask).wait_send()
@@ -263,9 +283,10 @@
         return carry
 
     lax.fori_loop(0, peers - 1, left, 0)
-    for mask in range(1, spread):
-        third(mask).wait()
-    last.wait()
+    for h in range(halves):
+        for mask in range(1, spread):
+            third(h, mask).wait()
+        last[h].wait()
 
 
 def run_layer(frames_in, slots, spread, norms, weights):
@@ -273,11 +294,11 @@
     frames, places, halves = rows * slots, patches // slots, 2
     piece = places // halves
     total = frames * places
-    vmem, hbm = pl.BlockSpec(memory_space=pltpu.VMEM), pl.BlockSpec(memory_space=pl.ANY)
+    vmem, hbm = pl.BlockSpec(memory_space=pltpu.VMEM), pl.BlockSpec(memory_space=pltpu.HBM)
     dma = pltpu.SemaphoreType.DMA
     return pl.pallas_call(
         functools.partial(layer_kernel, slots, spread),
-        out_shape=jax.ShapeDtypeStruct(frames_in.shape, BF16),
+        out_shape=jax.ShapeDtypeStruct((rows, slots, halves, piece, width), BF16),
         in_specs=[hbm] + [vmem] * 4 + [hbm] * 8,
         out_specs=hbm,
         scratch_shapes=[
@@ -286,7 +307,7 @@
             pltpu.VMEM((halves, frames, piece, width), BF16),
             pltpu.VMEM((total // piece, piece, width), BF16),
         ]
-        + [pltpu.VMEM((total, width), BF16)] * 5
+        + [pltpu.VMEM((total, width), BF16)] * 4
         + [
             dma((8,)),
             dma((halves,)),
@@ -294,8 +315,8 @@
             dma((halves, slots)),
             dma((halves, slots * spread)),
             dma((halves, slots * spread)),
-            dma((spread,)),
-            dma((spread,)),
+            dma((halves, spread)),
+            dma((halves, spread)),
         ],
         compiler_params=pltpu.CompilerParams(
             collective_id=0, has_side_effects=True, vmem_limit_bytes=60 << 20
@@ -304,7 +325,7 @@
         frames_in.reshape(rows, slots, halves, piece, width),
         *[norm.reshape(1, -1) for norm in norms],
         *weights,
-    )
+    ).reshape(frames_in.shape)
 
 
 def split_heads(tokens):

time: 82.9 us -> 80.5 us (0.971)
  Pallas kernels: 80.4 us -> 78 us
    pallas_call x1, Pallas kernels: 80.4 us -> 78 us  [run_layer(): pl.pallas_call(functools.partial(layer_kernel, slots, spread), out_shape=...]
where the time goes in v3:
time: 80.5 us; the launch traced here: 80.3 us
  Pallas kernels  78 us (97%)
  local copies, waits for them, and re-layouts  2.26 us (3%)
    pallas_call x1, Pallas kernels, run_layer(): pl.pallas_call(functools.partial(layer_kernel, slots, spread), out_shape=...  78 us
    unnamed x1, local copies, waits for them, and re-layouts  2.26 us

profile of v3, /device:TPU:0, one launch (start us, length us, event | category | flops | bytes accessed | tf_op | source)
XLA Modules:
  0.0 80.3 jit_solution(13955742200642388116)
XLA Ops:
  0.0 78.0 %shard_map.127 = bf16[8,4,2,8,1024]{4,3,2,1,0:T(8,128)(2,1)} custom-call(bf16[8,4,2,8,1024]{4,3,2,1,0:T(8,128)(2,1)} %bitcast.7, f32[1,1024]{1,0:T(1,128)} %bitcast.8, f32[1,1024]{1,0:T(1,128)} %bitcast.9, f32[1,1024]{1,0:T(1,128)} %bitcast.10, f32[1,1024]{1,0:T(1,128)} %bitcast.11, bf16[1024,1024]{1,0:T(8,128)(2,1)} %refs_0_.1, bf16[1024,1024]{1,0:T(8,128)(2,1)} %refs_1_.1, ...), custom_call_target="tpu_custom_call" | custom-call | tf_op jit(solution)/shard_map/pallas_call | solution.py:299
  78.0 2.3 %copy.15 = bf16[8,64,1024]{2,1,0:T(8,128)(2,1)} copy(bf16[8,64,1024]{2,1,0:T(8,128)(2,1)} %bitcast.6) | data formatting | bytes 2097152
